TPU v7x, 256 devices: a whole 4x4x8 slice. The times are simulated.
256 devices in a mesh: level: 4 (over y), sub: 16 (over z, core), rhs: 4 (over x).
Axes of the slice: x: 4, y: 4, z: 8, core: 2. Of those that a mesh axis runs over, the one named last changes fastest.
Arguments:
- rhs: float32 [4, 256, 256, 256], P('level', 'sub', 'rhs'), may hold values from -6 to 6
- lower_inv: bfloat16 [4, 256, 256, 256], P('level', 'sub'), may hold values from -0.25 to 2.1
- lower_off: bfloat16 [4, 256, 256, 256], P('level', 'sub'), may hold values from -0.25 to 0.25
- upper_inv: bfloat16 [4, 256, 256, 256], P('level', 'sub'), may hold values from -0.25 to 2.1
- upper_off: bfloat16 [4, 256, 256, 256], P('level', 'sub'), may hold values from -0.25 to 0.25
- ancestor: bfloat16 [256, 256, 256], P('sub', 'rhs'), may hold values from -6 to 6
- parent: int32 [3, 256], replicated, may hold values from 0 to 255, as said below
Outputs:
- solution: float32 [4, 256, 256, 256], P('level', 'sub', 'rhs')
- update: float32 [4, 256, 256, 256], P('level', 'sub', 'rhs')
Inputs may be any that keep to these rules, and one draw needn't show every extreme that they name: parent[t, c] names a supernode of sub index c // 16 or of sub index (c // 16) XOR 2 ** (t mod 4), where supernode s has sub index s // 16; a parent may have no children or several.
All inputs are finite; a program needn't handle non-finite values.
Results may differ from a plain program's by a relative error of at most 0.009.
Values may be sent and summed in bfloat16 or wider, within the bound.
A program may use at most 64 MiB of HBM per device.

v0:
```python
import jax
import jax.numpy as jnp
from jax import lax
from jax.sharding import PartitionSpec as P


def swapped(value, axis, apart):
    mask = 2**apart
    pairs = [(source, source ^ mask) for source in range(lax.axis_size(axis))]
    return lax.ppermute(value, axis, pairs)


def passed_along(value, axis, by):
    peers = lax.axis_size(axis)
    pairs = [(i, i + by) for i in range(peers) if 0 <= i + by < peers]
    return lax.ppermute(value, axis, pairs)


def block_product(left_rows, blocks):
    return lax.dot_general(
        left_rows, blocks, (((2,), (1,)), ((0,), (0,))), preferred_element_type=jnp.float32
    )


def forward_tier(residue, lower_inv, lower_off):
    forward = block_product(residue.astype(jnp.bfloat16), lower_inv).astype(jnp.bfloat16)
    return (forward, block_product(forward, lower_off))


def backward_tier(forward, above_rows, upper_inv, upper_off):
    reduced = forward.astype(jnp.float32) - block_product(above_rows, upper_off)
    return block_product(reduced.astype(jnp.bfloat16), upper_inv)


def parent_sums(selector, update):
    return jnp.einsum("jk,krw->jrw", selector, update, precision=lax.Precision.HIGHEST)


def fetch_parents(at_home, parent_slot, from_above, from_partner):
    home_rows = jnp.take(from_above, parent_slot, axis=0)
    partner_rows = jnp.take(from_partner, parent_slot, axis=0)
    return jnp.where(at_home[:, None, None], home_rows, partner_rows)


def body(rhs, lower_inv, lower_off, upper_inv, upper_off, ancestor, parent):
    levels = lax.axis_size("level")
    sub_count = lax.axis_size("sub")
    sub_bits = sub_count.bit_length() - 1
    tier_index = lax.axis_index("level")
    sub_index = lax.axis_index("sub")
    count_here = lower_inv.shape[1]
    rhs_here = rhs[0]
    lower_diag = lower_inv[0]
    lower_link = lower_off[0]
    upper_diag = upper_inv[0]
    upper_link = upper_off[0]
    parent_row = lax.dynamic_index_in_dim(
        parent, jnp.minimum(tier_index, levels - 2), 0, keepdims=False
    )
    parent_here = lax.dynamic_slice_in_dim(parent_row, sub_index * count_here, count_here)
    at_home = parent_here // count_here == sub_index
    parent_slot = parent_here % count_here
    slot_match = parent_slot[None, :] == jnp.arange(count_here, dtype=jnp.int32)[:, None]
    home_select = (slot_match & at_home[None, :]).astype(jnp.float32)
    far_select = (slot_match & jnp.logical_not(at_home)[None, :]).astype(jnp.float32)
    is_top = tier_index == levels - 1
    incoming = jnp.zeros(rhs_here.shape, jnp.float32)
    forward_keep = jnp.zeros(rhs_here.shape, jnp.bfloat16)
    update_keep = jnp.zeros(rhs_here.shape, jnp.float32)
    for section in range(levels):
        forward, update = forward_tier(rhs_here - incoming, lower_diag, lower_link)
        forward_keep = jnp.where(tier_index == section, forward, forward_keep)
        update_keep = jnp.where(tier_index == section, update, update_keep)
        if section + 1 < levels:
            home_part = parent_sums(home_select, update)
            far_part = parent_sums(far_select, update)
            received = swapped(far_part, "sub", section % sub_bits)
            incoming = passed_along(home_part + received, "level", 1)
    solution_keep = jnp.zeros(rhs_here.shape, jnp.float32)
    from_above = jnp.zeros(rhs_here.shape, jnp.bfloat16)
    from_partner = jnp.zeros(rhs_here.shape, jnp.bfloat16)
    for section in range(levels):
        tier_now = levels - 1 - section
        fetched = fetch_parents(at_home, parent_slot, from_above, from_partner)
        above_rows = jnp.where(is_top, ancestor, fetched)
        solution_part = backward_tier(forward_keep, above_rows, upper_diag, upper_link)
        solution_keep = jnp.where(tier_index == tier_now, solution_part, solution_keep)
        if section + 1 < levels:
            solution_bf = solution_part.astype(jnp.bfloat16)
            from_above = passed_along(solution_bf, "level", -1)
            from_partner = swapped(from_above, "sub", (tier_now - 1) % sub_bits)
    return (solution_keep[None], update_keep[None])


def solution(mesh):
    placed = (
        P("level", "sub", "rhs", None),
        P("level", "sub", None, None),
        P("level", "sub", None, None),
        P("level", "sub", None, None),
        P("level", "sub", None, None),
        P("sub", "rhs", None),
        P(),
    )
    return jax.shard_map(
        body,
        mesh=mesh,
        in_specs=placed,
        out_specs=(P("level", "sub", "rhs", None), P("level", "sub", "rhs", None)),
        check_vma=False,
    )
```

profile of v0, /device:TPU:1, one launch (start us, length us, event | category | flops | bytes accessed | tf_op | source)
XLA Modules:
  0.0 279.0 jit_solution(1580336746092555695)
XLA Ops:
  6.5 3.3 %collective-permute-start = (f32[16,64,256]{2,1,0:T(8,128)S(1)}, f32[16,64,256]{2,1,0:T(8,128)S(1)}, u32[]{:S(2)}, u32[]{:S(2)}) collective-permute-start(f32[16,64,256]{2,1,0:T(8,128)S(1)} %copy.11), channel_id=1, source_target_pairs={{0,4},{4,0},{8,12},{12,8},{16,20},{20,16},{24,28},{28,24},{32,36},... | collective-permute-start | bytes 3145736 | tf_op jit(solution)/shard_map/ppermute | solution.py:10
  14.2 22.1 %collective-permute-done.1 = f32[16,64,256]{2,1,0:T(8,128)S(1)} collective-permute-done((f32[16,64,256]{2,1,0:T(8,128)S(1)}, f32[16,64,256]{2,1,0:T(8,128)S(1)}, u32[]{:S(2)}, u32[]{:S(2)}) %collective-permute-start.1) | collective-permute-done | bytes 1048608 | tf_op jit(solution)/shard_map/ppermute | solution.py:16
  42.1 20.9 %collective-permute-done.2 = f32[16,64,256]{2,1,0:T(8,128)S(1)} collective-permute-done((f32[16,64,256]{2,1,0:T(8,128)S(1)}, f32[16,64,256]{2,1,0:T(8,128)S(1)}, u32[]{:S(2)}, u32[]{:S(2)}) %collective-permute-start.2) | collective-permute-done | bytes 1048608 | tf_op jit(solution)/shard_map/ppermute | solution.py:10
  63.7 4.4 %collective-permute-start.3 = (f32[16,64,256]{2,1,0:T(8,128)S(1)}, f32[16,64,256]{2,1,0:T(8,128)S(1)}, u32[]{:S(2)}, u32[]{:S(2)}) collective-permute-start(f32[16,64,256]{2,1,0:T(8,128)S(1)} %copy_add_fusion.1), channel_id=1, source_target_pairs={{0,64},{64,128},{128,192},{1,65},{65,129},{129,193},{2,66},{66,130... | collective-permute-start | bytes 3145736 | tf_op jit(solution)/shard_map/ppermute | solution.py:16
  68.1 20.2 %collective-permute-done.3 = f32[16,64,256]{2,1,0:T(8,128)S(1)} collective-permute-done((f32[16,64,256]{2,1,0:T(8,128)S(1)}, f32[16,64,256]{2,1,0:T(8,128)S(1)}, u32[]{:S(2)}, u32[]{:S(2)}) %collective-permute-start.3) | collective-permute-done | bytes 1048608 | tf_op jit(solution)/shard_map/ppermute | solution.py:16
  91.1 3.1 %collective-permute-start.4 = (f32[16,64,256]{2,1,0:T(8,128)S(1)}, f32[16,64,256]{2,1,0:T(8,128)S(1)}, u32[]{:S(2)}, u32[]{:S(2)}) collective-permute-start(f32[16,64,256]{2,1,0:T(8,128)S(1)} %copy.17), channel_id=1, source_target_pairs={{0,16},{4,20},{8,24},{12,28},{16,0},{20,4},{24,8},{28,12},{32,48},... | collective-permute-start | bytes 3145736 | tf_op jit(solution)/shard_map/ppermute | solution.py:10
  95.4 44.0 %collective-permute-done.4 = f32[16,64,256]{2,1,0:T(8,128)S(1)} collective-permute-done((f32[16,64,256]{2,1,0:T(8,128)S(1)}, f32[16,64,256]{2,1,0:T(8,128)S(1)}, u32[]{:S(2)}, u32[]{:S(2)}) %collective-permute-start.4) | collective-permute-done | bytes 1048608 | tf_op jit(solution)/shard_map/ppermute | solution.py:10
  141.0 5.1 %collective-permute-start.5 = (f32[16,64,256]{2,1,0:T(8,128)}, f32[16,64,256]{2,1,0:T(8,128)}, u32[]{:S(2)}, u32[]{:S(2)}) collective-permute-start(f32[16,64,256]{2,1,0:T(8,128)} %copy_add_fusion), channel_id=1, source_target_pairs={{0,64},{64,128},{128,192},{1,65},{65,129},{129,193},{2,66},{66,130... | collective-permute-start | bytes 3145736 | tf_op jit(solution)/shard_map/ppermute | solution.py:16
  149.4 17.1 %collective-permute-done.5 = f32[16,64,256]{2,1,0:T(8,128)} collective-permute-done((f32[16,64,256]{2,1,0:T(8,128)}, f32[16,64,256]{2,1,0:T(8,128)}, u32[]{:S(2)}, u32[]{:S(2)}) %collective-permute-start.5) | collective-permute-done | bytes 1048608 | tf_op jit(solution)/shard_map/ppermute | solution.py:16
  166.5 3.5 %select_select_fusion.6 = (bf16[16,64,256]{2,1,0:T(8,128)(2,1)}, bf16[16,64,256]{2,1,0:T(8,128)(2,1)}) fusion(bf16[16,64,256]{2,1,0:T(8,128)(2,1)} %copy-done.14, bf16[16,64,256]{2,1,0:T(8,128)(2,1)} %copy-done.13, bf16[16,64,256]{2,1,0:T(8,128)(2,1)} %copy-done.12, pred[]{:T(512)S(6)} %eq.63, pred[]{:T(512)S(6)} %eq.62, pred[]{:T(512)S(6)} %eq.55, ...), kind=kOutput, calls=%fused_computation.87 | convolution fusion | flops 136052736 | bytes 6815748 | tf_op jit(solution)/shard_map/dot_general | solution.py:20
  170.0 3.9 %fusion.180 = (bf16[16,64,256]{2,1,0:T(8,128)(2,1)}, f32[16,64,256]{2,1,0:T(8,128)}) fusion(bf16[1,16,256,256]{3,2,1,0:T(8,128)(2,1)S(1)} %copy-done, bf16[1,16,256,256]{3,2,1,0:T(8,128)(2,1)} %param.13, bf16[16,64,256]{2,1,0:T(8,128)(2,1)} %get-tuple-element.9, bf16[16,64,256]{2,1,0:T(8,128)(2,1)} %param.14, bf16[16,64,256]{2,1,0:T(8,128)(2,1)} %gather_fusion, ...), kind=kOutput, calls=%fused_computation.142 | convolution fusion | flops 270008320 | bytes 7340049 | tf_op jit(solution)/shard_map/dot_general | solution.py:20
  175.3 13.0 %collective-permute-done.6 = bf16[16,64,256]{2,1,0:T(8,128)(2,1)} collective-permute-done((bf16[16,64,256]{2,1,0:T(8,128)(2,1)}, bf16[16,64,256]{2,1,0:T(8,128)(2,1)}, u32[]{:S(2)}, u32[]{:S(2)}) %collective-permute-start.6) | collective-permute-done | bytes 524320 | tf_op jit(solution)/shard_map/ppermute | solution.py:16
  188.3 2.5 gather_fusion.1
  190.8 20.5 %collective-permute-done.7 = bf16[16,64,256]{2,1,0:T(8,128)(2,1)} collective-permute-done((bf16[16,64,256]{2,1,0:T(8,128)(2,1)}, bf16[16,64,256]{2,1,0:T(8,128)(2,1)}, u32[]{:S(2)}, u32[]{:S(2)}) %collective-permute-start.7) | collective-permute-done | bytes 524320 | tf_op jit(solution)/shard_map/ppermute | solution.py:10
  213.7 4.0 %fusion.183 = (bf16[16,64,256]{2,1,0:T(8,128)(2,1)}, f32[16,64,256]{2,1,0:T(8,128)}) fusion(bf16[1,16,256,256]{3,2,1,0:T(8,128)(2,1)S(1)} %copy-done, bf16[1,16,256,256]{3,2,1,0:T(8,128)(2,1)} %param.13, bf16[16,64,256]{2,1,0:T(8,128)(2,1)S(1)} %copy-done.8, bf16[16,64,256]{2,1,0:T(8,128)(2,1)S(1)} %copy-done.10, bf16[16,64,256]{2,1,0:T(8,128)(2,1)} %gather_fusion.2, ...), kind=kOutput, calls=%fused_computation.143 | convolution fusion | flops 270532608 | bytes 7864353 | tf_op jit(solution)/shard_map/dot_general | solution.py:20
  218.9 10.4 %collective-permute-done.8 = bf16[16,64,256]{2,1,0:T(8,128)(2,1)S(1)} collective-permute-done((bf16[16,64,256]{2,1,0:T(8,128)(2,1)}, bf16[16,64,256]{2,1,0:T(8,128)(2,1)S(1)}, u32[]{:S(2)}, u32[]{:S(2)}) %collective-permute-start.8) | collective-permute-done | bytes 524320 | tf_op jit(solution)/shard_map/ppermute | solution.py:16
  229.3 4.9 %collective-permute-start.9 = (bf16[16,64,256]{2,1,0:T(8,128)(2,1)S(1)}, bf16[16,64,256]{2,1,0:T(8,128)(2,1)S(1)}, u32[]{:S(2)}, u32[]{:S(2)}) collective-permute-start(bf16[16,64,256]{2,1,0:T(8,128)(2,1)S(1)} %collective-permute-done.8), channel_id=1, source_target_pairs={{0,8},{4,12},{8,0},{12,4},{16,24},{20,28},{24,16},{28,20},{32,40},... | collective-permute-start | bytes 1572872 | tf_op jit(solution)/shard_map/ppermute | solution.py:10
  235.6 9.2 %collective-permute-done.9 = bf16[16,64,256]{2,1,0:T(8,128)(2,1)S(1)} collective-permute-done((bf16[16,64,256]{2,1,0:T(8,128)(2,1)S(1)}, bf16[16,64,256]{2,1,0:T(8,128)(2,1)S(1)}, u32[]{:S(2)}, u32[]{:S(2)}) %collective-permute-start.9) | collective-permute-done | bytes 524320 | tf_op jit(solution)/shard_map/ppermute | solution.py:10
  246.2 4.2 %fusion.188 = (bf16[16,64,256]{2,1,0:T(8,128)(2,1)}, f32[16,64,256]{2,1,0:T(8,128)}) fusion(bf16[1,16,256,256]{3,2,1,0:T(8,128)(2,1)S(1)} %copy-done, bf16[1,16,256,256]{3,2,1,0:T(8,128)(2,1)} %param.13, bf16[16,64,256]{2,1,0:T(8,128)(2,1)} %get-tuple-element.9, bf16[16,64,256]{2,1,0:T(8,128)(2,1)} %param.14, bf16[16,64,256]{2,1,0:T(8,128)(2,1)} %gather_fusion.4, ...), kind=kOutput, calls=%fused_computation.144 | convolution fusion | flops 270532608 | bytes 7864353 | tf_op jit(solution)/shard_map/dot_general | solution.py:20
  251.6 12.1 %collective-permute-done.10 = bf16[16,64,256]{2,1,0:T(8,128)(2,1)} collective-permute-done((bf16[16,64,256]{2,1,0:T(8,128)(2,1)}, bf16[16,64,256]{2,1,0:T(8,128)(2,1)}, u32[]{:S(2)}, u32[]{:S(2)}) %collective-permute-start.10) | collective-permute-done | bytes 524320 | tf_op jit(solution)/shard_map/ppermute | solution.py:16
  263.7 3.2 %collective-permute-start.11 = (bf16[16,64,256]{2,1,0:T(8,128)(2,1)}, bf16[16,64,256]{2,1,0:T(8,128)(2,1)}, u32[]{:S(2)}, u32[]{:S(2)}) collective-permute-start(bf16[16,64,256]{2,1,0:T(8,128)(2,1)} %collective-permute-done.10), channel_id=1, source_target_pairs={{0,4},{4,0},{8,12},{12,8},{16,20},{20,16},{24,28},{28,24},{32,36},... | collective-permute-start | bytes 1572872 | tf_op jit(solution)/shard_map/ppermute | solution.py:10
  266.9 3.2 %fusion.35 = f32[1,16,64,256]{3,2,1,0:T(8,128)} fusion(bf16[16,64,256]{2,1,0:T(8,128)(2,1)} %get-tuple-element.10, bf16[1,16,256,256]{3,2,1,0:T(8,128)(2,1)} %param.11, f32[16,64,256]{2,1,0:T(8,128)} %copy-done.7, f32[16,64,256]{2,1,0:T(8,128)} %copy-done.6, f32[16,64,256]{2,1,0:T(8,128)S(1)} %copy-done.5, pred[]{:T(512)S(6)} %eq.63, pred[]{:T(512)S(6)} %eq.62, ...), kind=kOutput, calls=%fused_computation.44 | convolution fusion | flops 135266304 | bytes 6815748 | tf_op jit(solution)/shard_map/dot_general | solution.py:20
  270.1 2.5 gather_fusion.5
  275.1 3.9 %fusion.41 = f32[1,16,64,256]{3,2,1,0:T(8,128)} fusion(bf16[1,16,256,256]{3,2,1,0:T(8,128)(2,1)S(1)} %copy-done, f32[16,64,256]{2,1,0:T(8,128)} %get-tuple-element.16, f32[16,64,256]{2,1,0:T(8,128)} %get-tuple-element.14, f32[16,64,256]{2,1,0:T(8,128)} %get-tuple-element.12, bf16[1,16,256,256]{3,2,1,0:T(8,128)(2,1)} %param.13, ...), kind=kOutput, calls=%fused_computation.46 | convolution fusion | flops 271319040 | bytes 10485796 | tf_op jit(solution)/shard_map/dot_general | solution.py:20
  (68 shorter events, 37.0 us)
Async XLA Ops:
  0.6 169.3 %copy-start = (bf16[1,16,256,256]{3,2,1,0:T(8,128)(2,1)S(1)}, bf16[1,16,256,256]{3,2,1,0:T(8,128)(2,1)}, u32[]{:S(2)}) copy-start(bf16[1,16,256,256]{3,2,1,0:T(8,128)(2,1)} %param.12) | copy-start | bytes 6291460
  0.7 3.4 %copy-start.1 = (bf16[1,16,256,256]{3,2,1,0:T(8,128)(2,1)S(1)}, bf16[1,16,256,256]{3,2,1,0:T(8,128)(2,1)}, u32[]{:S(2)}) copy-start(bf16[1,16,256,256]{3,2,1,0:T(8,128)(2,1)} %param.11) | copy-start | bytes 6291460
  4.6 5.2 %copy-start.4 = (f32[16,64,256]{2,1,0:T(8,128)}, f32[16,64,256]{2,1,0:T(8,128)S(1)}, u32[]{:S(2)}) copy-start(f32[16,64,256]{2,1,0:T(8,128)S(1)} %fusion.22) | copy-start | bytes 3145732
  6.5 5.6 %collective-permute-start = (f32[16,64,256]{2,1,0:T(8,128)S(1)}, f32[16,64,256]{2,1,0:T(8,128)S(1)}, u32[]{:S(2)}, u32[]{:S(2)}) collective-permute-start(f32[16,64,256]{2,1,0:T(8,128)S(1)} %copy.11), channel_id=1, source_target_pairs={{0,4},{4,0},{8,12},{12,8},{16,20},{20,16},{24,28},{28,24},{32,36},... | collective-permute-start | bytes 3145736 | tf_op jit(solution)/shard_map/ppermute | solution.py:10
  11.0 25.3 %copy-start.2 = (bf16[1,16,256,256]{3,2,1,0:T(8,128)(2,1)S(1)}, bf16[1,16,256,256]{3,2,1,0:T(8,128)(2,1)}, u32[]{:S(2)}) copy-start(bf16[1,16,256,256]{3,2,1,0:T(8,128)(2,1)} %param.10) | copy-start | bytes 6291460
  11.0 25.3 %copy-start.3 = (f32[1,16,64,256]{3,2,1,0:T(8,128)S(1)}, f32[1,16,64,256]{3,2,1,0:T(8,128)}, u32[]{:S(2)}) copy-start(f32[1,16,64,256]{3,2,1,0:T(8,128)} %param.9) | copy-start | bytes 3145732
  12.7 23.6 %collective-permute-start.1 = (f32[16,64,256]{2,1,0:T(8,128)S(1)}, f32[16,64,256]{2,1,0:T(8,128)S(1)}, u32[]{:S(2)}, u32[]{:S(2)}) collective-permute-start(f32[16,64,256]{2,1,0:T(8,128)S(1)} %copy_add_fusion.2), channel_id=1, source_target_pairs={{0,64},{64,128},{128,192},{1,65},{65,129},{129,193},{2,66},{66,130... | collective-permute-start | bytes 3145736 | tf_op jit(solution)/shard_map/ppermute | solution.py:16
  37.3 3.6 %copy-start.6 = (f32[16,64,256]{2,1,0:T(8,128)}, f32[16,64,256]{2,1,0:T(8,128)S(1)}, u32[]{:S(2)}) copy-start(f32[16,64,256]{2,1,0:T(8,128)S(1)} %fusion.20) | copy-start | bytes 3145732
  39.2 23.9 %collective-permute-start.2 = (f32[16,64,256]{2,1,0:T(8,128)S(1)}, f32[16,64,256]{2,1,0:T(8,128)S(1)}, u32[]{:S(2)}, u32[]{:S(2)}) collective-permute-start(f32[16,64,256]{2,1,0:T(8,128)S(1)} %copy.14), channel_id=1, source_target_pairs={{0,8},{4,12},{8,0},{12,4},{16,24},{20,28},{24,16},{28,20},{32,40},... | collective-permute-start | bytes 3145736 | tf_op jit(solution)/shard_map/ppermute | solution.py:10
  63.7 24.6 %collective-permute-start.3 = (f32[16,64,256]{2,1,0:T(8,128)S(1)}, f32[16,64,256]{2,1,0:T(8,128)S(1)}, u32[]{:S(2)}, u32[]{:S(2)}) collective-permute-start(f32[16,64,256]{2,1,0:T(8,128)S(1)} %copy_add_fusion.1), channel_id=1, source_target_pairs={{0,64},{64,128},{128,192},{1,65},{65,129},{129,193},{2,66},{66,130... | collective-permute-start | bytes 3145736 | tf_op jit(solution)/shard_map/ppermute | solution.py:16
  89.3 4.9 %copy-start.7 = (f32[16,64,256]{2,1,0:T(8,128)}, f32[16,64,256]{2,1,0:T(8,128)S(1)}, u32[]{:S(2)}) copy-start(f32[16,64,256]{2,1,0:T(8,128)S(1)} %fusion.18) | copy-start | bytes 3145732
  91.1 48.3 %collective-permute-start.4 = (f32[16,64,256]{2,1,0:T(8,128)S(1)}, f32[16,64,256]{2,1,0:T(8,128)S(1)}, u32[]{:S(2)}, u32[]{:S(2)}) collective-permute-start(f32[16,64,256]{2,1,0:T(8,128)S(1)} %copy.17), channel_id=1, source_target_pairs={{0,16},{4,20},{8,24},{12,28},{16,0},{20,4},{24,8},{28,12},{32,48},... | collective-permute-start | bytes 3145736 | tf_op jit(solution)/shard_map/ppermute | solution.py:10
  141.0 25.5 %collective-permute-start.5 = (f32[16,64,256]{2,1,0:T(8,128)}, f32[16,64,256]{2,1,0:T(8,128)}, u32[]{:S(2)}, u32[]{:S(2)}) collective-permute-start(f32[16,64,256]{2,1,0:T(8,128)} %copy_add_fusion), channel_id=1, source_target_pairs={{0,64},{64,128},{128,192},{1,65},{65,129},{129,193},{2,66},{66,130... | collective-permute-start | bytes 3145736 | tf_op jit(solution)/shard_map/ppermute | solution.py:16
  173.8 39.8 %copy-start.8 = (bf16[16,64,256]{2,1,0:T(8,128)(2,1)S(1)}, bf16[16,64,256]{2,1,0:T(8,128)(2,1)}, u32[]{:S(2)}) copy-start(bf16[16,64,256]{2,1,0:T(8,128)(2,1)} %get-tuple-element.9) | copy-start | bytes 1572868
  173.8 39.8 %copy-start.10 = (bf16[16,64,256]{2,1,0:T(8,128)(2,1)S(1)}, bf16[16,64,256]{2,1,0:T(8,128)(2,1)}, u32[]{:S(2)}) copy-start(bf16[16,64,256]{2,1,0:T(8,128)(2,1)} %param.14) | copy-start | bytes 1572868
  173.8 14.5 %collective-permute-start.6 = (bf16[16,64,256]{2,1,0:T(8,128)(2,1)}, bf16[16,64,256]{2,1,0:T(8,128)(2,1)}, u32[]{:S(2)}, u32[]{:S(2)}) collective-permute-start(bf16[16,64,256]{2,1,0:T(8,128)(2,1)} %get-tuple-element.11), channel_id=1, source_target_pairs={{64,0},{128,64},{192,128},{65,1},{129,65},{193,129},{66,2},{130,66... | collective-permute-start | bytes 1572872 | tf_op jit(solution)/shard_map/ppermute | solution.py:16
  188.3 22.9 %collective-permute-start.7 = (bf16[16,64,256]{2,1,0:T(8,128)(2,1)}, bf16[16,64,256]{2,1,0:T(8,128)(2,1)}, u32[]{:S(2)}, u32[]{:S(2)}) collective-permute-start(bf16[16,64,256]{2,1,0:T(8,128)(2,1)} %collective-permute-done.6), channel_id=1, source_target_pairs={{0,16},{4,20},{8,24},{12,28},{16,0},{20,4},{24,8},{28,12},{32,48},... | collective-permute-start | bytes 1572872 | tf_op jit(solution)/shard_map/ppermute | solution.py:10
  217.7 11.6 %collective-permute-start.8 = (bf16[16,64,256]{2,1,0:T(8,128)(2,1)}, bf16[16,64,256]{2,1,0:T(8,128)(2,1)S(1)}, u32[]{:S(2)}, u32[]{:S(2)}) collective-permute-start(bf16[16,64,256]{2,1,0:T(8,128)(2,1)} %get-tuple-element.13), channel_id=1, source_target_pairs={{64,0},{128,64},{192,128},{65,1},{129,65},{193,129},{66,2},{130,66... | collective-permute-start | bytes 1572872 | tf_op jit(solution)/shard_map/ppermute | solution.py:16
  229.3 15.5 %collective-permute-start.9 = (bf16[16,64,256]{2,1,0:T(8,128)(2,1)S(1)}, bf16[16,64,256]{2,1,0:T(8,128)(2,1)S(1)}, u32[]{:S(2)}, u32[]{:S(2)}) collective-permute-start(bf16[16,64,256]{2,1,0:T(8,128)(2,1)S(1)} %collective-permute-done.8), channel_id=1, source_target_pairs={{0,8},{4,12},{8,0},{12,4},{16,24},{20,28},{24,16},{28,20},{32,40},... | collective-permute-start | bytes 1572872 | tf_op jit(solution)/shard_map/ppermute | solution.py:10
  246.2 20.7 %copy-start.5 = (f32[16,64,256]{2,1,0:T(8,128)S(1)}, f32[16,64,256]{2,1,0:T(8,128)}, u32[]{:S(2)}) copy-start(f32[16,64,256]{2,1,0:T(8,128)} %copy-done.4) | copy-start | bytes 3145732
  250.4 13.3 %collective-permute-start.10 = (bf16[16,64,256]{2,1,0:T(8,128)(2,1)}, bf16[16,64,256]{2,1,0:T(8,128)(2,1)}, u32[]{:S(2)}, u32[]{:S(2)}) collective-permute-start(bf16[16,64,256]{2,1,0:T(8,128)(2,1)} %get-tuple-element.15), channel_id=1, source_target_pairs={{64,0},{128,64},{192,128},{65,1},{129,65},{193,129},{66,2},{130,66... | collective-permute-start | bytes 1572872 | tf_op jit(solution)/shard_map/ppermute | solution.py:16
  263.7 9.0 %collective-permute-start.11 = (bf16[16,64,256]{2,1,0:T(8,128)(2,1)}, bf16[16,64,256]{2,1,0:T(8,128)(2,1)}, u32[]{:S(2)}, u32[]{:S(2)}) collective-permute-start(bf16[16,64,256]{2,1,0:T(8,128)(2,1)} %collective-permute-done.10), channel_id=1, source_target_pairs={{0,4},{4,0},{8,12},{12,8},{16,20},{20,16},{24,28},{28,24},{32,36},... | collective-permute-start | bytes 1572872 | tf_op jit(solution)/shard_map/ppermute | solution.py:10
  270.1 4.9 %copy-start.9 = (bf16[16,64,256]{2,1,0:T(8,128)(2,1)S(1)}, bf16[16,64,256]{2,1,0:T(8,128)(2,1)}, u32[]{:S(2)}) copy-start(bf16[16,64,256]{2,1,0:T(8,128)(2,1)} %get-tuple-element.9) | copy-start | bytes 1572868
  270.1 4.9 %copy-start.11 = (bf16[16,64,256]{2,1,0:T(8,128)(2,1)S(1)}, bf16[16,64,256]{2,1,0:T(8,128)(2,1)}, u32[]{:S(2)}) copy-start(bf16[16,64,256]{2,1,0:T(8,128)(2,1)} %param.14) | copy-start | bytes 1572868
  (3 other events, 5.2 us)
where the time goes:
time: 282 us; the launch traced here: 279 us
  waiting for transfers between devices  191 us (68%)
  matrix products  34.8 us (12%)
  starting transfers between devices  31.1 us (11%)
  local copies, waits for them, and re-layouts  17.8 us (6%)
  other arithmetic  3.86 us (1%)
    ppermute x6, waiting for transfers between devices, swapped(): return lax.ppermute(value, axis, pairs)  95.6 us
    ppermute x6, waiting for transfers between devices, passed_along(): return lax.ppermute(value, axis, pairs)  94.9 us
    dot_general x12, matrix products, block_product(): lax.dot_general(left_rows, blocks, (((2,), (1,)), ((0,), (0,))), preferre...  27.5 us
    ppermute x6, starting transfers between devices, swapped(): return lax.ppermute(value, axis, pairs)  16.2 us
    ppermute x6, starting transfers between devices, passed_along(): return lax.ppermute(value, axis, pairs)  14.9 us
    gather x4, local copies, waits for them, and re-layouts, fetch_parents(): home_rows = jnp.take(from_above, parent_slot, axis=0)  8.78 us
    dot_general x6, matrix products, parent_sums(): jnp.einsum('jk,krw->jrw', selector, update, precision=lax.Precision.HIGHEST)  7.25 us
    gather x3, local copies, waits for them, and re-layouts, fetch_parents(): partner_rows = jnp.take(from_partner, parent_slot, axis=0)  6.21 us
  transfers between devices with their start and end apart: 12, of which 11 were waited for; matrix products, arithmetic and copies ran while one was open for 6% of the time, Pallas kernels for 0%

commit v1 on v0

v1 whole, which is shorter than its diff:
```python
import functools

import jax
import jax.numpy as jnp
from jax import lax
from jax.experimental import pallas as pl
from jax.experimental.pallas import tpu as pltpu
from jax.sharding import PartitionSpec as P

MESH = pl.DeviceIdType.MESH
CHUNK = 8
LAG = 4


def other(sub, mask):
    return sub + mask - 2 * mask * ((sub // mask) % 2)


def kernel(
    parent, rhs_in, linv_in, loff_in, uinv_in, uoff_in, anc_in,
    sol_out, upd_out,
    rhs, linv, loff, uinv, uoff, anc, sol, upd,
    sel, res, fwd, snd, inc, crecv, hbuf, back, above, stage,
    in_sem, out_sem, fs, fr, bs, br, cs, cr,
):
    count, rows, width = rhs.shape
    size = CHUNK
    chunks = rows // size
    level = lax.axis_index("level")
    sub = lax.axis_index("sub")
    col = lax.axis_index("rhs")
    top = 3

    def at(lv, s):
        return (lv, s, col)

    def cut(k):
        return pl.ds(pl.multiple_of(k * size, size), size)

    loads = [
        pltpu.make_async_copy(rhs_in, rhs, in_sem.at[0]),
        pltpu.make_async_copy(linv_in, linv, in_sem.at[1]),
        pltpu.make_async_copy(loff_in, loff, in_sem.at[2]),
        pltpu.make_async_copy(uoff_in, uoff, in_sem.at[3]),
        pltpu.make_async_copy(uinv_in, uinv, in_sem.at[4]),
    ]
    for load in loads[:3]:
        load.start()

    def anc_load(k):
        return pltpu.make_async_copy(
            anc_in.at[:, cut(k), :], anc.at[k], in_sem.at[5 + k]
        )

    barrier = pltpu.get_barrier_semaphore()
    friends = {
        0: [(0, 1), (1, 0)],
        1: [(0, 0), (2, 0), (2, 2)],
        2: [(1, 0), (1, 2), (3, 0), (3, 4)],
        3: [(2, 0), (2, 4)],
    }
    for lv, group in friends.items():
        @pl.when(level == lv)
        def _():
            for to, mask in group:
                there = other(sub, mask) if mask else sub
                pl.semaphore_signal(
                    barrier, inc=1, device_id=at(to, there), device_id_type=MESH
                )

    row = jnp.minimum(level, top - 1)
    codes = []
    for c in range(count):
        p = parent[row, sub * count + c]
        codes.append((p % count) + jnp.where(p // count == sub, 0, count))
    lane = lax.broadcasted_iota(jnp.int32, (1, count * size), 1)
    target = jnp.zeros((1, count * size), jnp.int32)
    for c in range(count):
        target = jnp.where(lane // size == c, codes[c], target)
    target = target * size + lane % size
    down = lax.broadcasted_iota(jnp.int32, (2 * count * size, count * size), 0)
    sel[...] = (down == target).astype(jnp.bfloat16)

    for lv, group in friends.items():
        @pl.when(level == lv)
        def _():
            pl.semaphore_wait(barrier, len(group))

    def remote(src, dst, ss, rs, to):
        return pltpu.make_async_remote_copy(
            src_ref=src, dst_ref=dst, send_sem=ss, recv_sem=rs,
            device_id=to, device_id_type=MESH,
        )

    def up_home(k, lv):
        return remote(
            snd.at[k, pl.ds(0, count)], inc.at[k, pl.ds(0, count)],
            fs.at[k, 0], fr.at[k, 0], at(lv + 1, sub),
        )

    def up_far(k, lv):
        return remote(
            snd.at[k, pl.ds(count, count)], inc.at[k, pl.ds(count, count)],
            fs.at[k, 1], fr.at[k, 1], at(lv + 1, other(sub, 2**lv)),
        )

    def down_home(k, lv):
        return remote(
            back.at[k], above.at[k, pl.ds(0, count)],
            bs.at[k, 0], br.at[k, 0], at(lv - 1, sub),
        )

    def down_far(k, lv):
        return remote(
            back.at[k], above.at[k, pl.ds(count, count)],
            bs.at[k, 1], br.at[k, 1], at(lv - 1, other(sub, 2 ** (lv - 1))),
        )

    def side_up(k):
        return remote(
            snd.at[k, pl.ds(count, count)], crecv.at[k],
            cs.at[k, 0], cr.at[k, 0], at(0, other(sub, 1)),
        )

    def side_down(k):
        return remote(
            above.at[k, pl.ds(0, count)], above.at[k, pl.ds(count, count)],
            cs.at[k, 1], cr.at[k, 1], at(0, other(sub, 1)),
        )

    def upd_store(k):
        return pltpu.make_async_copy(
            upd.at[:, cut(k), :], upd_out.at[:, cut(k), :], out_sem.at[k, 0]
        )

    def sol_store(k):
        return pltpu.make_async_copy(
            sol.at[:, cut(k), :], sol_out.at[:, cut(k), :], out_sem.at[k, 1]
        )

    def forward(k):
        @pl.when(k == 0)
        def _():
            loads[0].wait()

        @pl.when(level == 0)
        def _():
            res[...] = rhs[:, cut(k), :].astype(jnp.bfloat16)

        @pl.when(level == 1)
        def _():
            up_home(k, 0).wait_recv()
            got = inc[k, pl.ds(0, count)].astype(jnp.float32)
            res[...] = (rhs[:, cut(k), :] - got).astype(jnp.bfloat16)

        @pl.when(level >= 2)
        def _():
            up_home(k, 1).wait_recv()
            up_far(k, 1).wait_recv()
            got = inc[k, pl.ds(0, count)].astype(jnp.float32)
            got = got + inc[k, pl.ds(count, count)].astype(jnp.float32)
            res[...] = (rhs[:, cut(k), :] - got).astype(jnp.bfloat16)

        @pl.when(k == 0)
        def _():
            loads[1].wait()

        for c in range(count):
            part = jnp.dot(res[c], linv[c], preferred_element_type=jnp.float32)
            fwd[k, c] = part.astype(jnp.bfloat16)

        @pl.when(k == 0)
        def _():
            loads[2].wait()
            for load in loads[3:]:
                load.start()

        @pl.when((k == 0) & (level == top))
        def _():
            for j in range(chunks):
                anc_load(j).start()

        for c in range(count):
            upd[c, cut(k), :] = jnp.dot(
                fwd[k, c], loff[c], preferred_element_type=jnp.float32
            )
        upd_store(k).start()

        @pl.when(level < top)
        def _():
            moved = upd[:, cut(k), :].reshape(count * size, width)
            both = jnp.dot(
                sel[...], moved.astype(jnp.bfloat16), preferred_element_type=jnp.float32
            ).reshape(2 * count, size, width)
            snd[k] = both.astype(jnp.bfloat16)
            hbuf[k] = both[:count]

        @pl.when(level == 0)
        def _():
            side_up(k).start()

        for lv in (1, 2):
            @pl.when(level == lv)
            def _():
                up_far(k, lv).start()
                up_home(k, lv).start()

    def settle(k):
        side_up(k).wait_recv()
        total = hbuf[k] + crecv[k].astype(jnp.float32)
        snd[k, pl.ds(0, count)] = total.astype(jnp.bfloat16)
        up_home(k, 0).start()

    def backward(k):
        @pl.when(k == 0)
        def _():
            for load in loads[3:]:
                load.wait()

        @pl.when(level == top)
        def _():
            anc_load(k).wait()
            stage[pl.ds(0, count)] = anc[k]

        @pl.when((level == 1) | (level == 2))
        def _():
            down_home(k, 2).wait_recv()
            down_far(k, 2).wait_recv()
            stage[...] = above[k]

        @pl.when(level == 0)
        def _():
            down_home(k, 1).wait_recv()
            side_down(k).start()
            side_down(k).wait_recv()
            stage[...] = above[k]

        for c in range(count):
            where = jnp.where(level == top, c, codes[c])
            term = jnp.dot(stage[where], uoff[c], preferred_element_type=jnp.float32)
            res[c] = (fwd[k, c].astype(jnp.float32) - term).astype(jnp.bfloat16)
        for c in range(count):
            part = jnp.dot(res[c], uinv[c], preferred_element_type=jnp.float32)
            sol[c, cut(k), :] = part
            back[k, c] = part.astype(jnp.bfloat16)
        for lv in (1, 2, 3):
            @pl.when(level == lv)
            def _():
                if lv > 1:
                    down_far(k, lv).start()
                down_home(k, lv).start()
        sol_store(k).start()

    lag = jnp.where(level == top, 0, jnp.where(level == 2, min(LAG, chunks), chunks))

    def step(i, carry):
        @pl.when(i < chunks)
        def _():
            forward(i)

        @pl.when((level == 0) & (i >= 1) & (i <= chunks))
        def _():
            settle(i - 1)

        @pl.when(i >= lag)
        def _():
            backward(i - lag)

        return carry

    lax.fori_loop(0, chunks + lag, step, 0)

    def finish(k, carry):
        upd_store(k).wait()
        sol_store(k).wait()

        @pl.when(level == 0)
        def _():
            side_up(k).wait_send()
            side_down(k).wait_send()

        for lv in (0, 1, 2):
            @pl.when(level == lv)
            def _():
                up_home(k, lv).wait_send()
                if lv > 0:
                    up_far(k, lv).wait_send()

        for lv in (1, 2, 3):
            @pl.when(level == lv)
            def _():
                down_home(k, lv).wait_send()
                if lv > 1:
                    down_far(k, lv).wait_send()

        return carry

    lax.fori_loop(0, chunks, finish, 0)


def body(rhs, lower_inv, lower_off, upper_inv, upper_off, ancestor, parent):
    count, rows, width = rhs.shape[1:]
    size = CHUNK
    chunks = rows // size
    f32, b16 = jnp.float32, jnp.bfloat16
    block = jax.ShapeDtypeStruct((count, rows, width), f32)
    vm = pltpu.VMEM
    sem = pltpu.SemaphoreType.DMA
    anyspace = pl.BlockSpec(memory_space=pl.ANY)
    sol, upd = pl.pallas_call(
        kernel,
        out_shape=(block, block),
        in_specs=[pl.BlockSpec(memory_space=pltpu.SMEM)] + [anyspace] * 6,
        out_specs=(anyspace, anyspace),
        scratch_shapes=[
            vm((count, rows, width), f32),
            vm((count, width, width), b16),
            vm((count, width, width), b16),
            vm((count, width, width), b16),
            vm((count, width, width), b16),
            vm((chunks, count, size, width), b16),
            vm((count, rows, width), f32),
            vm((count, rows, width), f32),
            vm((2 * count * size, count * size), b16),
            vm((count, size, width), b16),
            vm((chunks, count, size, width), b16),
            vm((chunks, 2 * count, size, width), b16),
            vm((chunks, 2 * count, size, width), b16),
            vm((chunks, count, size, width), b16),
            vm((chunks, count, size, width), f32),
            vm((chunks, count, size, width), b16),
            vm((chunks, 2 * count, size, width), b16),
            vm((2 * count, size, width), b16),
            sem((5 + chunks,)),
            sem((chunks, 2)),
            sem((chunks, 2)),
            sem((chunks, 2)),
            sem((chunks, 2)),
            sem((chunks, 2)),
            sem((chunks, 2)),
            sem((chunks, 2)),
        ],
        compiler_params=pltpu.CompilerParams(
            collective_id=0, has_side_effects=True, vmem_limit_bytes=40 * 2**20
        ),
        name="tree_solve",
    )(parent, rhs[0], lower_inv[0], lower_off[0], upper_inv[0], upper_off[0], ancestor)
    return (sol[None], upd[None])


def solution(mesh):
    placed = (
        P("level", "sub", "rhs", None),
        P("level", "sub", None, None),
        P("level", "sub", None, None),
        P("level", "sub", None, None),
        P("level", "sub", None, None),
        P("sub", "rhs", None),
        P(),
    )
    return jax.shard_map(
        body,
        mesh=mesh,
        in_specs=placed,
        out_specs=(P("level", "sub", "rhs", None), P("level", "sub", "rhs", None)),
        check_vma=False,
    )
```

time: 282 us -> 94.3 us (0.33)
  waiting for transfers between devices: 191 us -> 0 us
  Pallas kernels: 0 us -> 81.4 us
  matrix products: 34.8 us -> 0 us
  starting transfers between devices: 31.1 us -> 0 us
  local copies, waits for them, and re-layouts: 17.8 us -> 11.2 us
  other arithmetic: 3.86 us -> 0 us
    ppermute x12 -> x0, waiting for transfers between devices: 191 us -> none  [the longest x6 95.6 us: swapped(): return lax.ppermute(value, axis, pairs)]
    pallas_call x0 -> x1, Pallas kernels: none -> 81.4 us  [body(): pl.pallas_call(kernel, out_shape=(block, block), in_specs=[pl.BlockSpec(m...]
    dot_general x18 -> x0, matrix products: 34.8 us -> none  [the longest x12 27.5 us: block_product(): lax.dot_general(left_rows, blocks, (((2,), (1,)), ((0,), (0,))), preferre...]
    ppermute x12 -> x0, starting transfers between devices: 31.1 us -> none  [the longest x6 16.2 us: swapped(): return lax.ppermute(value, axis, pairs)]
    gather x7 -> x0, local copies, waits for them, and re-layouts: 15 us -> none  [the longest x4 8.78 us: fetch_parents(): home_rows = jnp.take(from_above, parent_slot, axis=0)]
    unnamed x30 -> x16, local copies, waits for them, and re-layouts: 0.07 us -> 11.2 us
    add x3 -> x0, other arithmetic: 2.88 us -> none  [body(): incoming = passed_along(home_part + received, 'level', 1)]
  transfers between devices with their start and end apart: 12 -> 0, of which waited for: 11 -> 0; matrix products, arithmetic and copies ran while one was open for 6% -> 0% of each run, Pallas kernels for 0% -> 0%
where the time goes in v1:
time: 94.3 us; the launch traced here: 93.3 us
  Pallas kernels  81.4 us (86%)
  local copies, waits for them, and re-layouts  11.2 us (12%)
    pallas_call x1, Pallas kernels, body(): pl.pallas_call(kernel, out_shape=(block, block), in_specs=[pl.BlockSpec(m...  81.4 us
    unnamed x16, local copies, waits for them, and re-layouts  11.2 us

profile of v1, /device:TPU:1, one launch (start us, length us, event | category | flops | bytes accessed | tf_op | source)
XLA Modules:
  0.0 93.3 jit_solution(15133915192990226852)
XLA Ops:
  0.6 0.0 copy-start
  0.6 1.6 %copy-done = bf16[1,16,256,256]{3,2,1,0:T(8,128)(2,1)S(1)} copy-done((bf16[1,16,256,256]{3,2,1,0:T(8,128)(2,1)S(1)}, bf16[1,16,256,256]{3,2,1,0:T(8,128)(2,1)}, u32[]{:S(2)}) %copy-start) | copy-done | bytes 2097176
  2.2 0.0 copy-start.1
  2.2 1.6 %copy-done.1 = bf16[1,16,256,256]{3,2,1,0:T(8,128)(2,1)S(1)} copy-done((bf16[1,16,256,256]{3,2,1,0:T(8,128)(2,1)S(1)}, bf16[1,16,256,256]{3,2,1,0:T(8,128)(2,1)}, u32[]{:S(2)}) %copy-start.1) | copy-done | bytes 2097176
  3.8 0.0 copy-start.2
  3.8 1.6 %copy-done.2 = bf16[1,16,256,256]{3,2,1,0:T(8,128)(2,1)S(1)} copy-done((bf16[1,16,256,256]{3,2,1,0:T(8,128)(2,1)S(1)}, bf16[1,16,256,256]{3,2,1,0:T(8,128)(2,1)}, u32[]{:S(2)}) %copy-start.2) | copy-done | bytes 2097176
  5.4 0.0 copy-start.3
  5.4 1.6 %copy-done.3 = bf16[1,16,256,256]{3,2,1,0:T(8,128)(2,1)S(1)} copy-done((bf16[1,16,256,256]{3,2,1,0:T(8,128)(2,1)S(1)}, bf16[1,16,256,256]{3,2,1,0:T(8,128)(2,1)}, u32[]{:S(2)}) %copy-start.3) | copy-done | bytes 2097176
  7.0 0.0 copy-start.4
  7.0 1.2 %copy-done.4 = f32[1,16,64,256]{3,2,1,0:T(8,128)S(1)} copy-done((f32[1,16,64,256]{3,2,1,0:T(8,128)S(1)}, f32[1,16,64,256]{3,2,1,0:T(8,128)}, u32[]{:S(2)}) %copy-start.4) | copy-done | bytes 1048600
  8.2 0.0 copy-start.5
  8.2 1.0 %copy-done.5 = bf16[16,64,256]{2,1,0:T(8,128)(2,1)S(1)} copy-done((bf16[16,64,256]{2,1,0:T(8,128)(2,1)S(1)}, bf16[16,64,256]{2,1,0:T(8,128)(2,1)}, u32[]{:S(2)}) %copy-start.5) | copy-done | bytes 524312
  9.3 0.0 copy-start.6
  9.3 0.7 copy-done.6
  10.0 81.4 %tree_solve.1 = (f32[16,64,256]{2,1,0:T(8,128)S(1)}, f32[16,64,256]{2,1,0:T(8,128)S(1)}) custom-call(s32[3,256]{1,0:T(4,128)S(1)} %copy-done.6, f32[16,64,256]{2,1,0:T(8,128)S(1)} %bitcast.11, bf16[16,256,256]{2,1,0:T(8,128)(2,1)S(1)} %bitcast.7, bf16[16,256,256]{2,1,0:T(8,128)(2,1)S(1)} %bitcast.8, bf16[16,256,256]{2,1,0:T(8,128)(2,1)S(1)} %bitcast.9, ...), custom_call_target="tpu_custom_call" | custom-call | tf_op jit(solution)/shard_map/tree_solve/pallas_call | solution.py:310
  91.3 1.0 %copy.11 = f32[1,16,64,256]{3,2,1,0:T(8,128)} copy(f32[1,16,64,256]{3,2,1,0:T(8,128)S(1)} %bitcast.13) | data formatting | bytes 2097152
  92.3 1.0 %copy.12 = f32[1,16,64,256]{3,2,1,0:T(8,128)} copy(f32[1,16,64,256]{3,2,1,0:T(8,128)S(1)} %bitcast.12) | data formatting | bytes 2097152
Async XLA Ops:
  0.6 1.6 %copy-start = (bf16[1,16,256,256]{3,2,1,0:T(8,128)(2,1)S(1)}, bf16[1,16,256,256]{3,2,1,0:T(8,128)(2,1)}, u32[]{:S(2)}) copy-start(bf16[1,16,256,256]{3,2,1,0:T(8,128)(2,1)} %param.8) | copy-start | bytes 6291460
  2.2 1.6 %copy-start.1 = (bf16[1,16,256,256]{3,2,1,0:T(8,128)(2,1)S(1)}, bf16[1,16,256,256]{3,2,1,0:T(8,128)(2,1)}, u32[]{:S(2)}) copy-start(bf16[1,16,256,256]{3,2,1,0:T(8,128)(2,1)} %param.9) | copy-start | bytes 6291460
  3.8 1.6 %copy-start.2 = (bf16[1,16,256,256]{3,2,1,0:T(8,128)(2,1)S(1)}, bf16[1,16,256,256]{3,2,1,0:T(8,128)(2,1)}, u32[]{:S(2)}) copy-start(bf16[1,16,256,256]{3,2,1,0:T(8,128)(2,1)} %param.10) | copy-start | bytes 6291460
  5.4 1.6 %copy-start.3 = (bf16[1,16,256,256]{3,2,1,0:T(8,128)(2,1)S(1)}, bf16[1,16,256,256]{3,2,1,0:T(8,128)(2,1)}, u32[]{:S(2)}) copy-start(bf16[1,16,256,256]{3,2,1,0:T(8,128)(2,1)} %param.11) | copy-start | bytes 6291460
  7.0 1.2 %copy-start.4 = (f32[1,16,64,256]{3,2,1,0:T(8,128)S(1)}, f32[1,16,64,256]{3,2,1,0:T(8,128)}, u32[]{:S(2)}) copy-start(f32[1,16,64,256]{3,2,1,0:T(8,128)} %param.7) | copy-start | bytes 3145732
  8.2 1.0 %copy-start.5 = (bf16[16,64,256]{2,1,0:T(8,128)(2,1)S(1)}, bf16[16,64,256]{2,1,0:T(8,128)(2,1)}, u32[]{:S(2)}) copy-start(bf16[16,64,256]{2,1,0:T(8,128)(2,1)} %anc_in.1) | copy-start | bytes 1572868
  9.3 0.7 copy-start.6

commit v2 on v1

--- a/solution.py
+++ b/solution.py
@@ -10,6 +10,25 @@
 MESH = pl.DeviceIdType.MESH
 CHUNK = 8
 LAG = 4
+UP_SIDE = ('all', 'all', 'all')
+DOWN_SIDE = ('all', 'none', 'none')
+
+
+def chosen(rule, k):
+    if rule in ("all", "none"):
+        return rule == "all"
+    return k % 2 == (1 if rule == "odd" else 0)
+
+
+def gate(condition, yes, no=None):
+    if condition is True or condition is False:
+        pick = yes if condition else no
+        if pick is not None:
+            pick()
+        return
+    pl.when(condition)(yes)
+    if no is not None:
+        pl.when(jnp.logical_not(condition))(no)
 
 
 def other(sub, mask):
@@ -55,8 +74,8 @@
     barrier = pltpu.get_barrier_semaphore()
     friends = {
         0: [(0, 1), (1, 0)],
-        1: [(0, 0), (2, 0), (2, 2)],
-        2: [(1, 0), (1, 2), (3, 0), (3, 4)],
+        1: [(0, 0), (1, 2), (2, 0), (2, 2)],
+        2: [(1, 0), (1, 2), (2, 4), (3, 0), (3, 4)],
         3: [(2, 0), (2, 4)],
     }
     for lv, group in friends.items():
@@ -116,16 +135,16 @@
             bs.at[k, 1], br.at[k, 1], at(lv - 1, other(sub, 2 ** (lv - 1))),
         )
 
-    def side_up(k):
+    def side_up(k, lv):
         return remote(
             snd.at[k, pl.ds(count, count)], crecv.at[k],
-            cs.at[k, 0], cr.at[k, 0], at(0, other(sub, 1)),
-        )
-
-    def side_down(k):
+            cs.at[k, 0], cr.at[k, 0], at(lv, other(sub, 2**lv)),
+        )
+
+    def side_down(k, lv):
         return remote(
             above.at[k, pl.ds(0, count)], above.at[k, pl.ds(count, count)],
-            cs.at[k, 1], cr.at[k, 1], at(0, other(sub, 1)),
+            cs.at[k, 1], cr.at[k, 1], at(lv, other(sub, 2**lv)),
         )
 
     def upd_store(k):
@@ -153,13 +172,21 @@
             got = inc[k, pl.ds(0, count)].astype(jnp.float32)
             res[...] = (rhs[:, cut(k), :] - got).astype(jnp.bfloat16)
 
-        @pl.when(level >= 2)
-        def _():
-            up_home(k, 1).wait_recv()
-            up_far(k, 1).wait_recv()
-            got = inc[k, pl.ds(0, count)].astype(jnp.float32)
-            got = got + inc[k, pl.ds(count, count)].astype(jnp.float32)
-            res[...] = (rhs[:, cut(k), :] - got).astype(jnp.bfloat16)
+        for lv in (2, 3):
+            @pl.when(level == lv)
+            def _():
+                up_home(k, lv - 1).wait_recv()
+                got = inc[k, pl.ds(0, count)].astype(jnp.float32)
+
+                def both():
+                    up_far(k, lv - 1).wait_recv()
+                    more = got + inc[k, pl.ds(count, count)].astype(jnp.float32)
+                    res[...] = (rhs[:, cut(k), :] - more).astype(jnp.bfloat16)
+
+                def single():
+                    res[...] = (rhs[:, cut(k), :] - got).astype(jnp.bfloat16)
+
+                gate(chosen(UP_SIDE[lv - 1], k), single, both)
 
         @pl.when(k == 0)
         def _():
@@ -195,21 +222,33 @@
             snd[k] = both.astype(jnp.bfloat16)
             hbuf[k] = both[:count]
 
-        @pl.when(level == 0)
-        def _():
-            side_up(k).start()
-
-        for lv in (1, 2):
-            @pl.when(level == lv)
-            def _():
-                up_far(k, lv).start()
-                up_home(k, lv).start()
-
-    def settle(k):
-        side_up(k).wait_recv()
+        for lv in (0, 1, 2):
+            @pl.when(level == lv)
+            def _():
+                def straight():
+                    up_far(k, lv).start()
+                    up_home(k, lv).start()
+
+                gate(
+                    chosen(UP_SIDE[lv], k),
+                    lambda: side_up(k, lv).start(), straight,
+                )
+
+    def settle(k, lv):
+        side_up(k, lv).wait_recv()
         total = hbuf[k] + crecv[k].astype(jnp.float32)
         snd[k, pl.ds(0, count)] = total.astype(jnp.bfloat16)
-        up_home(k, 0).start()
+        up_home(k, lv).start()
+
+    def relay(k):
+        for lv in (0, 1, 2):
+            def go():
+                down_home(k, lv + 1).wait_recv()
+                side_down(k, lv).start()
+
+            @pl.when(level == lv)
+            def _():
+                gate(chosen(DOWN_SIDE[lv], k), go)
 
     def backward(k):
         @pl.when(k == 0)
@@ -222,18 +261,18 @@
             anc_load(k).wait()
             stage[pl.ds(0, count)] = anc[k]
 
-        @pl.when((level == 1) | (level == 2))
-        def _():
-            down_home(k, 2).wait_recv()
-            down_far(k, 2).wait_recv()
-            stage[...] = above[k]
-
-        @pl.when(level == 0)
-        def _():
-            down_home(k, 1).wait_recv()
-            side_down(k).start()
-            side_down(k).wait_recv()
-            stage[...] = above[k]
+        for lv in (0, 1, 2):
+            def straight():
+                down_home(k, lv + 1).wait_recv()
+                down_far(k, lv + 1).wait_recv()
+
+            @pl.when(level == lv)
+            def _():
+                gate(
+                    chosen(DOWN_SIDE[lv], k),
+                    lambda: side_down(k, lv).wait_recv(), straight,
+                )
+                stage[...] = above[k]
 
         for c in range(count):
             where = jnp.where(level == top, c, codes[c])
@@ -246,52 +285,63 @@
         for lv in (1, 2, 3):
             @pl.when(level == lv)
             def _():
-                if lv > 1:
-                    down_far(k, lv).start()
                 down_home(k, lv).start()
+                gate(
+                    chosen(DOWN_SIDE[lv - 1], k),
+                    lambda: None, lambda: down_far(k, lv).start(),
+                )
         sol_store(k).start()
 
-    lag = jnp.where(level == top, 0, jnp.where(level == 2, min(LAG, chunks), chunks))
+    lag = jnp.where(level == top, -1, jnp.where(level == 2, min(LAG, chunks), chunks))
 
     def step(i, carry):
         @pl.when(i < chunks)
         def _():
             forward(i)
 
-        @pl.when((level == 0) & (i >= 1) & (i <= chunks))
-        def _():
-            settle(i - 1)
-
-        @pl.when(i >= lag)
-        def _():
-            backward(i - lag)
+        for lv in (0, 1, 2):
+            @pl.when((level == lv) & (i >= 1) & (i <= chunks))
+            def _():
+                gate(chosen(UP_SIDE[lv], i - 1), lambda: settle(i - 1, lv))
+
+        @pl.when((i >= lag) & (i < chunks + lag))
+        def _():
+            relay(i - lag)
+
+        @pl.when(i > lag)
+        def _():
+            backward(i - lag - 1)
 
         return carry
 
-    lax.fori_loop(0, chunks + lag, step, 0)
+    lax.fori_loop(0, chunks + lag + 1, step, 0)
 
     def finish(k, carry):
         upd_store(k).wait()
         sol_store(k).wait()
 
-        @pl.when(level == 0)
-        def _():
-            side_up(k).wait_send()
-            side_down(k).wait_send()
-
         for lv in (0, 1, 2):
             @pl.when(level == lv)
             def _():
                 up_home(k, lv).wait_send()
-                if lv > 0:
-                    up_far(k, lv).wait_send()
+                gate(
+                    chosen(UP_SIDE[lv], k),
+                    lambda: side_up(k, lv).wait_send(),
+                    lambda: up_far(k, lv).wait_send(),
+                )
+                gate(
+                    chosen(DOWN_SIDE[lv], k),
+                    lambda: side_down(k, lv).wait_send(),
+                )
 
         for lv in (1, 2, 3):
             @pl.when(level == lv)
             def _():
                 down_home(k, lv).wait_send()
-                if lv > 1:
-                    down_far(k, lv).wait_send()
+                gate(
+                    chosen(DOWN_SIDE[lv - 1], k),
+                    lambda: None, lambda: down_far(k, lv).wait_send(),
+                )
 
         return carry
 
@@ -341,7 +391,7 @@
             sem((chunks, 2)),
         ],
         compiler_params=pltpu.CompilerParams(
-            collective_id=0, has_side_effects=True, vmem_limit_bytes=40 * 2**20
+            collective_id=0, has_side_effects=True, vmem_limit_bytes=62 * 2**20
         ),
         name="tree_solve",
     )(parent, rhs[0], lower_inv[0], lower_off[0], upper_inv[0], upper_off[0], ancestor)

time: 94.3 us -> 73.7 us (0.78)
  Pallas kernels: 81.4 us -> 69.5 us
  local copies, waits for them, and re-layouts: 11.2 us -> 3.36 us
    pallas_call x1, Pallas kernels: 81.4 us -> 69.5 us  [body(): pl.pallas_call(kernel, out_shape=(block, block), in_specs=[pl.BlockSpec(m...]
    unnamed x16 -> x4, local copies, waits for them, and re-layouts: 11.2 us -> 3.36 us
where the time goes in v2:
time: 73.7 us; the launch traced here: 73.5 us
  Pallas kernels  69.5 us (94%)
  local copies, waits for them, and re-layouts  3.36 us (5%)
    pallas_call x1, Pallas kernels, body(): pl.pallas_call(kernel, out_shape=(block, block), in_specs=[pl.BlockSpec(m...  69.5 us
    unnamed x4, local copies, waits for them, and re-layouts  3.36 us

profile of v2, /device:TPU:1, one launch (start us, length us, event | category | flops | bytes accessed | tf_op | source)
XLA Modules:
  0.0 73.5 jit_solution(285512980250454649)
XLA Ops:
  0.6 69.5 %tree_solve.1 = (f32[16,64,256]{2,1,0:T(8,128)}, f32[16,64,256]{2,1,0:T(8,128)}) custom-call(s32[3,256]{1,0:T(4,128)} %parent.1, f32[16,64,256]{2,1,0:T(8,128)} %bitcast.11, bf16[16,256,256]{2,1,0:T(8,128)(2,1)} %bitcast.7, bf16[16,256,256]{2,1,0:T(8,128)(2,1)} %bitcast.8, bf16[16,256,256]{2,1,0:T(8,128)(2,1)} %bitcast.9, bf16[16,256,256]{2,1,0:T(8,128)(2,1)} %bitcast.10, ...), custom_call_target="tpu_custom_call" | custom-call | tf_op jit(solution)/shard_map/tree_solve/pallas_call | solution.py:360
  70.2 0.0 copy-start
  70.2 2.4 %copy.11 = f32[1,16,64,256]{3,2,1,0:T(8,128)} copy(f32[1,16,64,256]{3,2,1,0:T(8,128)} %bitcast.13) | data formatting | bytes 2097152
  72.6 0.0 copy-done
  72.6 1.0 %copy.12 = f32[1,16,64,256]{3,2,1,0:T(8,128)} copy(f32[1,16,64,256]{3,2,1,0:T(8,128)S(1)} %bitcast.12) | data formatting | bytes 2097152
Async XLA Ops:
  70.2 2.4 %copy-start = (f32[16,64,256]{2,1,0:T(8,128)S(1)}, f32[16,64,256]{2,1,0:T(8,128)}, u32[]{:S(2)}) copy-start(f32[16,64,256]{2,1,0:T(8,128)} %get-tuple-element.5) | copy-start | bytes 3145732

commit v3 on v1

--- a/solution.py
+++ b/solution.py
@@ -21,7 +21,7 @@
     sol_out, upd_out,
     rhs, linv, loff, uinv, uoff, anc, sol, upd,
     sel, res, fwd, snd, inc, crecv, hbuf, back, above, stage,
-    in_sem, out_sem, fs, fr, bs, br, cs, cr,
+    in_sem, piece_sem, out_sem, fs, fr, bs, br, cs, cr,
 ):
     count, rows, width = rhs.shape
     size = CHUNK
@@ -38,14 +38,30 @@
         return pl.ds(pl.multiple_of(k * size, size), size)
 
     loads = [
-        pltpu.make_async_copy(rhs_in, rhs, in_sem.at[0]),
-        pltpu.make_async_copy(linv_in, linv, in_sem.at[1]),
-        pltpu.make_async_copy(loff_in, loff, in_sem.at[2]),
         pltpu.make_async_copy(uoff_in, uoff, in_sem.at[3]),
         pltpu.make_async_copy(uinv_in, uinv, in_sem.at[4]),
     ]
-    for load in loads[:3]:
-        load.start()
+    first = pltpu.make_async_copy(
+        rhs_in.at[:, cut(0), :], rhs.at[:, cut(0), :], in_sem.at[0]
+    )
+    later = pl.ds(size, rows - size)
+    rest = pltpu.make_async_copy(
+        rhs_in.at[:, later, :], rhs.at[:, later, :], in_sem.at[1]
+    )
+    quarter = count // 4
+    pieces = []
+    for i, (source, target) in enumerate(((linv_in, linv), (loff_in, loff))):
+        for j in range(4):
+            where = pl.ds(j * quarter, quarter)
+            pieces.append(
+                pltpu.make_async_copy(
+                    source.at[where], target.at[where], piece_sem.at[i, j]
+                )
+            )
+    first.start()
+    for piece in pieces:
+        piece.start()
+    rest.start()
 
     def anc_load(k):
         return pltpu.make_async_copy(
@@ -55,8 +71,8 @@
     barrier = pltpu.get_barrier_semaphore()
     friends = {
         0: [(0, 1), (1, 0)],
-        1: [(0, 0), (2, 0), (2, 2)],
-        2: [(1, 0), (1, 2), (3, 0), (3, 4)],
+        1: [(0, 0), (1, 2), (2, 0), (2, 2)],
+        2: [(1, 0), (1, 2), (2, 4), (3, 0), (3, 4)],
         3: [(2, 0), (2, 4)],
     }
     for lv, group in friends.items():
@@ -94,14 +110,7 @@
 
     def up_home(k, lv):
         return remote(
-            snd.at[k, pl.ds(0, count)], inc.at[k, pl.ds(0, count)],
-            fs.at[k, 0], fr.at[k, 0], at(lv + 1, sub),
-        )
-
-    def up_far(k, lv):
-        return remote(
-            snd.at[k, pl.ds(count, count)], inc.at[k, pl.ds(count, count)],
-            fs.at[k, 1], fr.at[k, 1], at(lv + 1, other(sub, 2**lv)),
+            snd.at[k, 0], inc.at[k], fs.at[k], fr.at[k], at(lv + 1, sub),
         )
 
     def down_home(k, lv):
@@ -116,10 +125,10 @@
             bs.at[k, 1], br.at[k, 1], at(lv - 1, other(sub, 2 ** (lv - 1))),
         )
 
-    def side_up(k):
-        return remote(
-            snd.at[k, pl.ds(count, count)], crecv.at[k],
-            cs.at[k, 0], cr.at[k, 0], at(0, other(sub, 1)),
+    def side_up(k, lv):
+        return remote(
+            snd.at[k, 1], crecv.at[k],
+            cs.at[k, 0], cr.at[k, 0], at(lv, other(sub, 2**lv)),
         )
 
     def side_down(k):
@@ -141,29 +150,26 @@
     def forward(k):
         @pl.when(k == 0)
         def _():
-            loads[0].wait()
+            first.wait()
+
+        @pl.when(k == 1)
+        def _():
+            rest.wait()
 
         @pl.when(level == 0)
         def _():
             res[...] = rhs[:, cut(k), :].astype(jnp.bfloat16)
 
-        @pl.when(level == 1)
+        @pl.when(level > 0)
         def _():
             up_home(k, 0).wait_recv()
-            got = inc[k, pl.ds(0, count)].astype(jnp.float32)
+            got = inc[k].astype(jnp.float32)
             res[...] = (rhs[:, cut(k), :] - got).astype(jnp.bfloat16)
 
-        @pl.when(level >= 2)
-        def _():
-            up_home(k, 1).wait_recv()
-            up_far(k, 1).wait_recv()
-            got = inc[k, pl.ds(0, count)].astype(jnp.float32)
-            got = got + inc[k, pl.ds(count, count)].astype(jnp.float32)
-            res[...] = (rhs[:, cut(k), :] - got).astype(jnp.bfloat16)
-
         @pl.when(k == 0)
         def _():
-            loads[1].wait()
+            for piece in pieces[:4]:
+                piece.wait()
 
         for c in range(count):
             part = jnp.dot(res[c], linv[c], preferred_element_type=jnp.float32)
@@ -171,8 +177,9 @@
 
         @pl.when(k == 0)
         def _():
-            loads[2].wait()
-            for load in loads[3:]:
+            for piece in pieces[4:]:
+                piece.wait()
+            for load in loads:
                 load.start()
 
         @pl.when((k == 0) & (level == top))
@@ -189,32 +196,34 @@
         @pl.when(level < top)
         def _():
             moved = upd[:, cut(k), :].reshape(count * size, width)
-            both = jnp.dot(
-                sel[...], moved.astype(jnp.bfloat16), preferred_element_type=jnp.float32
-            ).reshape(2 * count, size, width)
-            snd[k] = both.astype(jnp.bfloat16)
-            hbuf[k] = both[:count]
-
-        @pl.when(level == 0)
-        def _():
-            side_up(k).start()
-
-        for lv in (1, 2):
-            @pl.when(level == lv)
-            def _():
-                up_far(k, lv).start()
-                up_home(k, lv).start()
-
-    def settle(k):
-        side_up(k).wait_recv()
+            moved = moved.astype(jnp.bfloat16)
+
+            def sums(half):
+                rows_of = sel[pl.ds(half * count * size, count * size)]
+                total = jnp.dot(rows_of, moved, preferred_element_type=jnp.float32)
+                return total.reshape(count, size, width)
+
+            snd[k, 1] = sums(1).astype(jnp.bfloat16)
+            for lv in (0, 1, 2):
+                @pl.when(level == lv)
+                def _():
+                    side_up(k, lv).start()
+            hbuf[k] = sums(0)
+
+    def settle(k, lv):
+        side_up(k, lv).wait_recv()
         total = hbuf[k] + crecv[k].astype(jnp.float32)
-        snd[k, pl.ds(0, count)] = total.astype(jnp.bfloat16)
-        up_home(k, 0).start()
+        snd[k, 0] = total.astype(jnp.bfloat16)
+        up_home(k, lv).start()
+
+    def relay(k):
+        down_home(k, 1).wait_recv()
+        side_down(k).start()
 
     def backward(k):
         @pl.when(k == 0)
         def _():
-            for load in loads[3:]:
+            for load in loads:
                 load.wait()
 
         @pl.when(level == top)
@@ -230,8 +239,6 @@
 
         @pl.when(level == 0)
         def _():
-            down_home(k, 1).wait_recv()
-            side_down(k).start()
             side_down(k).wait_recv()
             stage[...] = above[k]
 
@@ -246,45 +253,46 @@
         for lv in (1, 2, 3):
             @pl.when(level == lv)
             def _():
+                down_home(k, lv).start()
                 if lv > 1:
                     down_far(k, lv).start()
-                down_home(k, lv).start()
         sol_store(k).start()
 
-    lag = jnp.where(level == top, 0, jnp.where(level == 2, min(LAG, chunks), chunks))
+    lag = jnp.where(level == top, -1, jnp.where(level == 2, min(LAG, chunks), chunks))
 
     def step(i, carry):
         @pl.when(i < chunks)
         def _():
             forward(i)
 
-        @pl.when((level == 0) & (i >= 1) & (i <= chunks))
-        def _():
-            settle(i - 1)
-
-        @pl.when(i >= lag)
-        def _():
-            backward(i - lag)
+        for lv in (0, 1, 2):
+            @pl.when((level == lv) & (i >= 1) & (i <= chunks))
+            def _():
+                settle(i - 1, lv)
+
+        @pl.when((level == 0) & (i >= lag) & (i < chunks + lag))
+        def _():
+            relay(i - lag)
+
+        @pl.when(i > lag)
+        def _():
+            backward(i - lag - 1)
 
         return carry
 
-    lax.fori_loop(0, chunks + lag, step, 0)
+    lax.fori_loop(0, chunks + lag + 1, step, 0)
 
     def finish(k, carry):
         upd_store(k).wait()
         sol_store(k).wait()
-
-        @pl.when(level == 0)
-        def _():
-            side_up(k).wait_send()
-            side_down(k).wait_send()
 
         for lv in (0, 1, 2):
             @pl.when(level == lv)
             def _():
                 up_home(k, lv).wait_send()
-                if lv > 0:
-                    up_far(k, lv).wait_send()
+                side_up(k, lv).wait_send()
+                if lv == 0:
+                    side_down(k).wait_send()
 
         for lv in (1, 2, 3):
             @pl.when(level == lv)
@@ -303,13 +311,12 @@
     size = CHUNK
     chunks = rows // size
     f32, b16 = jnp.float32, jnp.bfloat16
-    block = jax.ShapeDtypeStruct((count, rows, width), f32)
     vm = pltpu.VMEM
     sem = pltpu.SemaphoreType.DMA
     anyspace = pl.BlockSpec(memory_space=pl.ANY)
     sol, upd = pl.pallas_call(
         kernel,
-        out_shape=(block, block),
+        out_shape=(vm((count, rows, width), f32), vm((count, rows, width), f32)),
         in_specs=[pl.BlockSpec(memory_space=pltpu.SMEM)] + [anyspace] * 6,
         out_specs=(anyspace, anyspace),
         scratch_shapes=[
@@ -324,24 +331,25 @@
             vm((2 * count * size, count * size), b16),
             vm((count, size, width), b16),
             vm((chunks, count, size, width), b16),
-            vm((chunks, 2 * count, size, width), b16),
-            vm((chunks, 2 * count, size, width), b16),
+            vm((chunks, 2, count, size, width), b16),
+            vm((chunks, count, size, width), b16),
             vm((chunks, count, size, width), b16),
             vm((chunks, count, size, width), f32),
             vm((chunks, count, size, width), b16),
             vm((chunks, 2 * count, size, width), b16),
             vm((2 * count, size, width), b16),
             sem((5 + chunks,)),
-            sem((chunks, 2)),
-            sem((chunks, 2)),
-            sem((chunks, 2)),
+            sem((2, 4)),
+            sem((chunks, 2)),
+            sem((chunks,)),
+            sem((chunks,)),
             sem((chunks, 2)),
             sem((chunks, 2)),
             sem((chunks, 2)),
             sem((chunks, 2)),
         ],
         compiler_params=pltpu.CompilerParams(
-            collective_id=0, has_side_effects=True, vmem_limit_bytes=40 * 2**20
+            collective_id=0, has_side_effects=True, vmem_limit_bytes=58 * 2**20
         ),
         name="tree_solve",
     )(parent, rhs[0], lower_inv[0], lower_off[0], upper_inv[0], upper_off[0], ancestor)

time: 94.3 us -> 71.4 us (0.76); the launches traced: 93.3 us -> 71.3 us
  Pallas kernels: 81.4 us -> 68.7 us
  local copies, waits for them, and re-layouts: 11.2 us -> 1.94 us
    pallas_call x1, Pallas kernels: 81.4 us -> 68.7 us  [body(): pl.pallas_call(kernel, out_shape=(vm((count, rows, width), f32), vm((coun...]
    unnamed x16 -> x2, local copies, waits for them, and re-layouts: 11.2 us -> 1.94 us
where the time goes in v3:
time: 71.4 us; the launch traced here: 71.3 us
  Pallas kernels  68.7 us (96%)
  local copies, waits for them, and re-layouts  1.94 us (3%)
    pallas_call x1, Pallas kernels, body(): pl.pallas_call(kernel, out_shape=(vm((count, rows, width), f32), vm((coun...  68.7 us
    unnamed x2, local copies, waits for them, and re-layouts  1.94 us

profile of v3, /device:TPU:1, one launch (start us, length us, event | category | flops | bytes accessed | tf_op | source)
XLA Modules:
  0.0 71.3 jit_solution(4007692708183481512)
XLA Ops:
  0.6 68.7 %tree_solve.1 = (f32[16,64,256]{2,1,0:T(8,128)S(1)}, f32[16,64,256]{2,1,0:T(8,128)S(1)}) custom-call(s32[3,256]{1,0:T(4,128)} %parent.1, f32[16,64,256]{2,1,0:T(8,128)} %bitcast.13, bf16[16,256,256]{2,1,0:T(8,128)(2,1)} %bitcast.9, bf16[16,256,256]{2,1,0:T(8,128)(2,1)} %bitcast.10, bf16[16,256,256]{2,1,0:T(8,128)(2,1)} %bitcast.11, ...), custom_call_target="tpu_custom_call" | custom-call | tf_op jit(solution)/shard_map/tree_solve/pallas_call | solution.py:317
  69.4 1.0 %copy.11 = f32[1,16,64,256]{3,2,1,0:T(8,128)} copy(f32[1,16,64,256]{3,2,1,0:T(8,128)S(1)} %bitcast.8) | data formatting | bytes 2097152
  70.4 1.0 %copy.12 = f32[1,16,64,256]{3,2,1,0:T(8,128)} copy(f32[1,16,64,256]{3,2,1,0:T(8,128)S(1)} %bitcast.7) | data formatting | bytes 2097152

commit v4 on v3

--- a/solution.py
+++ b/solution.py
@@ -97,11 +97,6 @@
     down = lax.broadcasted_iota(jnp.int32, (2 * count * size, count * size), 0)
     sel[...] = (down == target).astype(jnp.bfloat16)
 
-    for lv, group in friends.items():
-        @pl.when(level == lv)
-        def _():
-            pl.semaphore_wait(barrier, len(group))
-
     def remote(src, dst, ss, rs, to):
         return pltpu.make_async_remote_copy(
             src_ref=src, dst_ref=dst, send_sem=ss, recv_sem=rs,
@@ -192,6 +187,11 @@
                 fwd[k, c], loff[c], preferred_element_type=jnp.float32
             )
         upd_store(k).start()
+
+        for lv, group in friends.items():
+            @pl.when((k == 0) & (level == lv))
+            def _():
+                pl.semaphore_wait(barrier, len(group))
 
         @pl.when(level < top)
         def _():
@@ -253,9 +253,9 @@
         for lv in (1, 2, 3):
             @pl.when(level == lv)
             def _():
-                down_home(k, lv).start()
                 if lv > 1:
                     down_far(k, lv).start()
+                down_home(k, lv).start()
         sol_store(k).start()
 
     lag = jnp.where(level == top, -1, jnp.where(level == 2, min(LAG, chunks), chunks))

time: 71.4 us -> 71.2 us (level)
  no operation moved by 1% of the time
where the time goes in v4:
time: 71.2 us; the launch traced here: 71.1 us
  Pallas kernels  68.5 us (96%)
  local copies, waits for them, and re-layouts  1.94 us (3%)
    pallas_call x1, Pallas kernels, body(): pl.pallas_call(kernel, out_shape=(vm((count, rows, width), f32), vm((coun...  68.5 us
    unnamed x2, local copies, waits for them, and re-layouts  1.94 us

profile of v4, /device:TPU:1, one launch (start us, length us, event | category | flops | bytes accessed | tf_op | source)
XLA Modules:
  0.0 71.1 jit_solution(1421375690240647270)
XLA Ops:
  0.6 68.5 %tree_solve.1 = (f32[16,64,256]{2,1,0:T(8,128)S(1)}, f32[16,64,256]{2,1,0:T(8,128)S(1)}) custom-call(s32[3,256]{1,0:T(4,128)} %parent.1, f32[16,64,256]{2,1,0:T(8,128)} %bitcast.13, bf16[16,256,256]{2,1,0:T(8,128)(2,1)} %bitcast.9, bf16[16,256,256]{2,1,0:T(8,128)(2,1)} %bitcast.10, bf16[16,256,256]{2,1,0:T(8,128)(2,1)} %bitcast.11, ...), custom_call_target="tpu_custom_call" | custom-call | tf_op jit(solution)/shard_map/tree_solve/pallas_call | solution.py:317
  69.2 1.0 %copy.11 = f32[1,16,64,256]{3,2,1,0:T(8,128)} copy(f32[1,16,64,256]{3,2,1,0:T(8,128)S(1)} %bitcast.8) | data formatting | bytes 2097152
  70.2 1.0 %copy.12 = f32[1,16,64,256]{3,2,1,0:T(8,128)} copy(f32[1,16,64,256]{3,2,1,0:T(8,128)S(1)} %bitcast.7) | data formatting | bytes 2097152
